TPU v7x, 128 devices: a whole 4x4x4 slice. The times are simulated.
128 devices in a mesh: pair: 2 (over x_hi), gx: 8 (over y, x_lo), gy: 8 (over z, core).
Axes of the slice: x: 4 (x_hi: 2, x_lo: 2; x = x_hi * 2 + x_lo), y: 4, z: 4, core: 2. Of those that a mesh axis runs over, the one named last changes fastest.
Arguments:
- sound_speed_sq: float32 [64, 64, 1024], P('gx', 'gy'), may hold values from 0.5 to 2
- wind_profile: float32 [3, 1024], replicated, may hold values from -0.6 to 0.6
- forward_field: bfloat16 [4, 4, 64, 64, 1024], P(None, None, 'gx', 'gy'), may hold values from -6 to 6
- adjoint_state: float32 [2, 4, 64, 64, 1024], P('pair', None, 'gx', 'gy'), may hold values from -0.3125 to 0.3125
- pair_counts: int32 [2], P('pair'), may hold values from 64 to 256, as said below
- source_cells: int32 [512, 3], P('pair'), may hold values from 0 to 1023, as said below
- receiver_cells: int32 [512, 3], P('pair'), may hold values from 0 to 1023, as said below
- residuals: float32 [512, 4], P('pair'), may hold values from -16 to 16
Outputs:
- kernels: float32 [4, 64, 64, 1024], P(None, 'gx', 'gy', 'pair')
- final_state: float32 [2, 4, 64, 64, 1024], P('pair', None, 'gx', 'gy')
Inputs may be any that keep to these rules, and one draw needn't show every extreme that they name: `pair_counts`: one group in every draw has exactly 256 live pairs. `source_cells`: columns are the cell along the first, second and third dimension, each within the grid. `receiver_cells`: columns are the cell along the first, second and third dimension, each within the grid; several pairs may share a cell.
All inputs are finite; a program needn't handle non-finite values.
Results may differ from a plain program's by a relative error of at most 0.00115.
Values may be sent and summed in bfloat16 or wider, within the bound.
A program may use at most 128 MiB of HBM per device.

v0:
```python
import jax
import jax.numpy as jnp
from jax import lax
from jax.sharding import PartitionSpec as P

step_length = 0.25


def extended(shard, sides, width):
    for axis, dim in sides:
        size, length = (lax.axis_size(axis), shard.shape[dim])
        up = [(i, (i + 1) % size) for i in range(size - 1)]
        down = [(j, i) for i, j in up]
        last = lax.slice_in_dim(shard, length - width, length, axis=dim)
        initial = lax.slice_in_dim(shard, 0, width, axis=dim)
        before = lax.ppermute(last, axis, up)
        after = lax.ppermute(initial, axis, down)
        shard = jnp.concatenate([before, shard, after], axis=dim)
    return shard


def central(padded):
    dims = padded.ndim
    east_diff = (padded[..., 2:, 1:-1, :] - padded[..., :-2, 1:-1, :]) * 0.5
    north_diff = (padded[..., 1:-1, 2:, :] - padded[..., 1:-1, :-2, :]) * 0.5
    center = padded[..., 1:-1, 1:-1, :]
    vertical = jnp.pad(center, [(0, 0)] * (dims - 1) + [(1, 1)])
    up_diff = (vertical[..., 2:] - vertical[..., :-2]) * 0.5
    return (east_diff, north_diff, up_diff, center)


def local_flat(cells, width_x, width_y, depth):
    local_x = cells[:, 0] - lax.axis_index("gx") * width_x
    local_y = cells[:, 1] - lax.axis_index("gy") * width_y
    inside = (local_x >= 0) & (local_x < width_x) & (local_y >= 0) & (local_y < width_y)
    flat = (
        jnp.clip(local_x, 0, width_x - 1) * width_y + jnp.clip(local_y, 0, width_y - 1)
    ) * depth + cells[:, 2]
    return (flat, inside.astype(jnp.float32))


def shards(
    sound_speed_sq,
    wind_profile,
    forward_field,
    adjoint_state,
    pair_counts,
    source_cells,
    receiver_cells,
    residuals,
):
    steps_total = forward_field.shape[0]
    width_x, width_y, depth = sound_speed_sq.shape
    slots = residuals.shape[0]
    east_wind = wind_profile[0]
    north_wind = wind_profile[1]
    vertical_wind = wind_profile[2]
    live = (jnp.arange(slots, dtype=jnp.int32) < pair_counts[0]).astype(jnp.float32)
    src_flat, src_inside = local_flat(source_cells, width_x, width_y, depth)
    rcv_flat, rcv_inside = local_flat(receiver_cells, width_x, width_y, depth)
    pressure_snaps = forward_field[:, 0].reshape(steps_total, -1)
    local_samples = (
        jnp.take(pressure_snaps, src_flat, axis=1).astype(jnp.float32) * src_inside[None, :]
    )
    samples = lax.psum(local_samples, ("gx", "gy"))
    state = adjoint_state[0]
    kernel_local = jnp.zeros((4, width_x, width_y, depth), jnp.float32)
    for step in range(steps_total):
        snap = steps_total - 1 - step
        amplitude = residuals[:, snap] * samples[snap] * live * rcv_inside
        injected = (
            jnp.zeros((width_x * width_y * depth,), jnp.float32)
            .at[rcv_flat]
            .add(amplitude)
            .reshape(width_x, width_y, depth)
        )
        padded = extended(state, (("gx", 1), ("gy", 2)), 1)
        east_diff, north_diff, up_diff, center = central(padded)
        pressure = center[0]
        velocity = center[1:]
        divergence = east_diff[1] + north_diff[2] + up_diff[3]
        p_new = (
            pressure
            + step_length
            * (
                sound_speed_sq * divergence
                + east_wind * east_diff[0]
                + north_wind * north_diff[0]
                + vertical_wind * up_diff[0]
            )
            + injected
        )
        p_padded = extended(p_new, (("gx", 0), ("gy", 1)), 1)
        p_east, p_north, p_up, unused_center = central(p_padded)
        gradient = jnp.stack([p_east, p_north, p_up])
        a_new = velocity + step_length * (
            gradient
            + east_wind * east_diff[1:]
            + north_wind * north_diff[1:]
            + vertical_wind * up_diff[1:]
        )
        forward_rim = extended(forward_field[snap], (("gx", 1), ("gy", 2)), 1).astype(jnp.float32)
        f_east, f_north, f_up, unused_forward = central(forward_rim)
        pieces = [p_new * (f_east[1] + f_north[2] + f_up[3])]
        for along in (f_east, f_north, f_up):
            pieces.append(
                p_new * along[0] + a_new[0] * along[1] + a_new[1] * along[2] + a_new[2] * along[3]
            )
        increment = jnp.stack(pieces)
        kernel_local = kernel_local + increment
        state = jnp.concatenate([p_new[None], a_new], axis=0)
    kernels = lax.psum_scatter(kernel_local, "pair", scatter_dimension=3, tiled=True)
    return (kernels, state[None])


def solution(mesh):
    in_specs = (
        P("gx", "gy", None),
        P(),
        P(None, None, "gx", "gy", None),
        P("pair", None, "gx", "gy", None),
        P("pair"),
        P("pair", None),
        P("pair", None),
        P("pair", None),
    )
    out_specs = (P(None, "gx", "gy", "pair"), P("pair", None, "gx", "gy", None))
    return jax.shard_map(shards, mesh=mesh, in_specs=in_specs, out_specs=out_specs, check_vma=False)
```

profile of v0, /device:TPU:1, one launch (start us, length us, event | category | flops | bytes accessed | tf_op | source)
XLA Modules:
  0.0 556.1 jit_solution(320897750737244086)
XLA Ops:
  11.0 5.2 collective-permute-start.4
  17.0 3.7 collective-permute-start.1
  26.9 13.0 %copy.11 = bf16[4,1,8,8,1024]{0,4,3,2,1:T(8,128)(2,1)} copy(bf16[4,1,8,8,1024]{4,3,2,1,0:T(8,128)(2,1)} %slice.831) | data formatting | bytes 1048576 | tf_op jit(solution)/shard_map/slice | solution.py:61
  40.0 8.7 %gather_fusion = bf16[256,4]{1,0:T(8,128)(2,1)S(1)} fusion(bf16[4,65536]{0,1:T(8,128)(2,1)} %bitcast.532, s32[1024]{0:T(1024)S(1)} %pad_clamp_fusion), kind=kCustom, calls=%fused_computation | custom fusion | bytes 5120 | tf_op jit(solution)/shard_map/jit(_take)/gather | solution.py:63
  48.8 278.8 %psum.7 = f32[4,256]{0,1:T(8,128)S(1)} all-reduce(f32[4,256]{0,1:T(8,128)S(1)} %multiply_bitcast_fusion), channel_id=1, replica_groups=mesh['pair'=2,'gx'=8,'gy'=8] {'gx','gy'}, use_global_device_ids=true, to_apply=%region_0.1 | all-reduce | flops 1024 | bytes 8192 | tf_op jit(solution)/shard_map/psum | solution.py:65
  349.0 4.0 collective-permute-start.28
  355.5 4.0 collective-permute-start.40
  359.5 9.9 %collective-permute-start.7 = (bf16[4,10,1,1024]{3,2,1,0:T(2,128)(2,1)S(1)}, bf16[4,10,1,1024]{3,2,1,0:T(2,128)(2,1)S(1)}, u32[]{:S(2)}, u32[]{:S(2)}) collective-permute-start(bf16[4,10,1,1024]{3,2,1,0:T(2,128)(2,1)S(1)} %get-tuple-element.75), channel_id=1, source_target_pairs={{1,0},{2,1},{3,2},{4,3},{5,4},{6,5},{7,6},{9,8},{10,9},{11,10},{12... | collective-permute-start | bytes 245768 | tf_op jit(solution)/shard_map/ppermute | solution.py:17
  380.5 3.6 collective-permute-start.3
  389.1 3.8 collective-permute-start.30
  404.4 5.1 collective-permute-start.11
  423.9 3.3 collective-permute-start.15
  429.9 4.0 collective-permute-done.14
  442.6 3.2 collective-permute-start.23
  456.3 3.8 collective-permute-done.24
  460.3 3.3 collective-permute-start.27
  467.1 3.2 collective-permute-done.26
  479.1 3.2 collective-permute-start.35
  484.4 3.2 collective-permute-done.34
  492.8 3.8 collective-permute-done.36
  496.8 4.3 collective-permute-start.39
  503.3 4.4 collective-permute-done.38
  521.4 3.2 collective-permute-done.46
  528.4 20.9 %reduce-scatter.2.cloned.1.call-done = f32[4,8,8,512]{3,2,1,0:T(8,128)} async-done(((f32[4,8,8,1024]{3,2,1,0:T(8,128)}), f32[4,8,8,512]{3,2,1,0:T(8,128)}) %reduce-scatter.2.cloned.1.call-update) | async-done | bytes 524304 | tf_op jit(solution)/shard_map/reduce_scatter | solution.py:112
  (178 shorter events, 136.9 us)
Async XLA Ops:
  7.2 542.1 %reduce-scatter.2.cloned.1.call-start = ((), (), s32[]{:S(2)}) async-start(), calls=%async_computation.1 | async-start | bytes 1572864 | tf_op jit(solution)/shard_map/reduce_scatter | solution.py:112
  9.7 335.5 %collective-permute-start.5 = (bf16[4,1,8,1024]{3,2,1,0:T(8,128)(2,1)}, bf16[4,1,8,1024]{3,2,1,0:T(8,128)(2,1)}, u32[]{:S(2)}, u32[]{:S(2)}) collective-permute-start(bf16[4,1,8,1024]{3,2,1,0:T(8,128)(2,1)} %get-tuple-element.83), channel_id=1, source_target_pairs={{8,0},{16,8},{24,16},{32,24},{40,32},{48,40},{56,48},{9,1},{17,9},... | collective-permute-start | bytes 196616 | tf_op jit(solution)/shard_map/ppermute | solution.py:17
  11.0 335.5 %collective-permute-start.4 = (bf16[4,1,8,1024]{3,2,1,0:T(8,128)(2,1)}, bf16[4,1,8,1024]{3,2,1,0:T(8,128)(2,1)}, u32[]{:S(2)}, u32[]{:S(2)}) collective-permute-start(bf16[4,1,8,1024]{3,2,1,0:T(8,128)(2,1)} %get-tuple-element.82), channel_id=1, source_target_pairs={{0,8},{8,16},{16,24},{24,32},{32,40},{40,48},{48,56},{1,9},{9,17},... | collective-permute-start | bytes 196616 | tf_op jit(solution)/shard_map/ppermute | solution.py:16
  17.0 357.2 %collective-permute-start.1 = (f32[4,1,8,1024]{3,2,1,0:T(8,128)}, f32[4,1,8,1024]{3,2,1,0:T(8,128)S(1)}, u32[]{:S(2)}, u32[]{:S(2)}) collective-permute-start(f32[4,1,8,1024]{3,2,1,0:T(8,128)} %get-tuple-element.66), channel_id=1, source_target_pairs={{0,8},{8,16},{16,24},{24,32},{32,40},{40,48},{48,56},{1,9},{9,17},... | collective-permute-start | bytes 393224 | tf_op jit(solution)/shard_map/ppermute | solution.py:16
  20.6 356.7 %collective-permute-start = (f32[4,1,8,1024]{3,2,1,0:T(8,128)}, f32[4,1,8,1024]{3,2,1,0:T(8,128)}, u32[]{:S(2)}, u32[]{:S(2)}) collective-permute-start(f32[4,1,8,1024]{3,2,1,0:T(8,128)} %get-tuple-element.67), channel_id=1, source_target_pairs={{8,0},{16,8},{24,16},{32,24},{40,32},{48,40},{56,48},{9,1},{17,9},... | collective-permute-start | bytes 393224 | tf_op jit(solution)/shard_map/ppermute | solution.py:17
  22.6 326.4 %collective-permute-start.17 = (bf16[4,1,8,1024]{3,2,1,0:T(8,128)(2,1)}, bf16[4,1,8,1024]{3,2,1,0:T(8,128)(2,1)}, u32[]{:S(2)}, u32[]{:S(2)}) collective-permute-start(bf16[4,1,8,1024]{3,2,1,0:T(8,128)(2,1)} %get-tuple-element.81), channel_id=1, source_target_pairs={{8,0},{16,8},{24,16},{32,24},{40,32},{48,40},{56,48},{9,1},{17,9},... | collective-permute-start | bytes 196616 | tf_op jit(solution)/shard_map/ppermute | solution.py:17
  345.2 7.8 %collective-permute-start.16 = (bf16[4,1,8,1024]{3,2,1,0:T(8,128)(2,1)}, bf16[4,1,8,1024]{3,2,1,0:T(8,128)(2,1)S(1)}, u32[]{:S(2)}, u32[]{:S(2)}) collective-permute-start(bf16[4,1,8,1024]{3,2,1,0:T(8,128)(2,1)} %get-tuple-element.80), channel_id=1, source_target_pairs={{0,8},{8,16},{16,24},{24,32},{32,40},{40,48},{48,56},{1,9},{9,17},... | collective-permute-start | bytes 196616 | tf_op jit(solution)/shard_map/ppermute | solution.py:16
  346.5 8.9 %collective-permute-start.29 = (bf16[4,1,8,1024]{3,2,1,0:T(8,128)(2,1)}, bf16[4,1,8,1024]{3,2,1,0:T(8,128)(2,1)S(1)}, u32[]{:S(2)}, u32[]{:S(2)}) collective-permute-start(bf16[4,1,8,1024]{3,2,1,0:T(8,128)(2,1)} %get-tuple-element.79), channel_id=1, source_target_pairs={{8,0},{16,8},{24,16},{32,24},{40,32},{48,40},{56,48},{9,1},{17,9},... | collective-permute-start | bytes 196616 | tf_op jit(solution)/shard_map/ppermute | solution.py:17
  349.0 10.5 %collective-permute-start.28 = (bf16[4,1,8,1024]{3,2,1,0:T(8,128)(2,1)}, bf16[4,1,8,1024]{3,2,1,0:T(8,128)(2,1)S(1)}, u32[]{:S(2)}, u32[]{:S(2)}) collective-permute-start(bf16[4,1,8,1024]{3,2,1,0:T(8,128)(2,1)} %get-tuple-element.78), channel_id=1, source_target_pairs={{0,8},{8,16},{16,24},{24,32},{32,40},{40,48},{48,56},{1,9},{9,17},... | collective-permute-start | bytes 196616 | tf_op jit(solution)/shard_map/ppermute | solution.py:16
  353.0 16.6 %collective-permute-start.41 = (bf16[4,1,8,1024]{3,2,1,0:T(8,128)(2,1)}, bf16[4,1,8,1024]{3,2,1,0:T(8,128)(2,1)S(1)}, u32[]{:S(2)}, u32[]{:S(2)}) collective-permute-start(bf16[4,1,8,1024]{3,2,1,0:T(8,128)(2,1)} %get-tuple-element.77), channel_id=1, source_target_pairs={{8,0},{16,8},{24,16},{32,24},{40,32},{48,40},{56,48},{9,1},{17,9},... | collective-permute-start | bytes 196616 | tf_op jit(solution)/shard_map/ppermute | solution.py:17
  355.5 16.0 %collective-permute-start.40 = (bf16[4,1,8,1024]{3,2,1,0:T(8,128)(2,1)}, bf16[4,1,8,1024]{3,2,1,0:T(8,128)(2,1)S(1)}, u32[]{:S(2)}, u32[]{:S(2)}) collective-permute-start(bf16[4,1,8,1024]{3,2,1,0:T(8,128)(2,1)} %get-tuple-element.76), channel_id=1, source_target_pairs={{0,8},{8,16},{16,24},{24,32},{32,40},{40,48},{48,56},{1,9},{9,17},... | collective-permute-start | bytes 196616 | tf_op jit(solution)/shard_map/ppermute | solution.py:16
  359.5 21.0 %collective-permute-start.7 = (bf16[4,10,1,1024]{3,2,1,0:T(2,128)(2,1)S(1)}, bf16[4,10,1,1024]{3,2,1,0:T(2,128)(2,1)S(1)}, u32[]{:S(2)}, u32[]{:S(2)}) collective-permute-start(bf16[4,10,1,1024]{3,2,1,0:T(2,128)(2,1)S(1)} %get-tuple-element.75), channel_id=1, source_target_pairs={{1,0},{2,1},{3,2},{4,3},{5,4},{6,5},{7,6},{9,8},{10,9},{11,10},{12... | collective-permute-start | bytes 245768 | tf_op jit(solution)/shard_map/ppermute | solution.py:17
  369.6 14.5 %collective-permute-start.6 = (bf16[4,10,1,1024]{3,2,1,0:T(2,128)(2,1)S(1)}, bf16[4,10,1,1024]{3,2,1,0:T(2,128)(2,1)S(1)}, u32[]{:S(2)}, u32[]{:S(2)}) collective-permute-start(bf16[4,10,1,1024]{3,2,1,0:T(2,128)(2,1)S(1)} %get-tuple-element.74), channel_id=1, source_target_pairs={{0,1},{1,2},{2,3},{3,4},{4,5},{5,6},{6,7},{8,9},{9,10},{10,11},{11... | collective-permute-start | bytes 245768 | tf_op jit(solution)/shard_map/ppermute | solution.py:16
  371.5 25.6 %collective-permute-start.19 = (bf16[4,10,1,1024]{3,2,1,0:T(2,128)(2,1)S(1)}, bf16[4,10,1,1024]{3,2,1,0:T(2,128)(2,1)S(1)}, u32[]{:S(2)}, u32[]{:S(2)}) collective-permute-start(bf16[4,10,1,1024]{3,2,1,0:T(2,128)(2,1)S(1)} %get-tuple-element.73), channel_id=1, source_target_pairs={{1,0},{2,1},{3,2},{4,3},{5,4},{6,5},{7,6},{9,8},{10,9},{11,10},{12... | collective-permute-start | bytes 245768 | tf_op jit(solution)/shard_map/ppermute | solution.py:17
  374.2 25.5 %collective-permute-start.18 = (bf16[4,10,1,1024]{3,2,1,0:T(2,128)(2,1)S(1)}, bf16[4,10,1,1024]{3,2,1,0:T(2,128)(2,1)S(1)}, u32[]{:S(2)}, u32[]{:S(2)}) collective-permute-start(bf16[4,10,1,1024]{3,2,1,0:T(2,128)(2,1)S(1)} %get-tuple-element.72), channel_id=1, source_target_pairs={{0,1},{1,2},{2,3},{3,4},{4,5},{5,6},{6,7},{8,9},{9,10},{10,11},{11... | collective-permute-start | bytes 245768 | tf_op jit(solution)/shard_map/ppermute | solution.py:16
  377.3 50.0 %collective-permute-start.31 = (bf16[4,10,1,1024]{3,2,1,0:T(2,128)(2,1)S(1)}, bf16[4,10,1,1024]{3,2,1,0:T(2,128)(2,1)S(1)}, u32[]{:S(2)}, u32[]{:S(2)}) collective-permute-start(bf16[4,10,1,1024]{3,2,1,0:T(2,128)(2,1)S(1)} %get-tuple-element.71), channel_id=1, source_target_pairs={{1,0},{2,1},{3,2},{4,3},{5,4},{6,5},{7,6},{9,8},{10,9},{11,10},{12... | collective-permute-start | bytes 245768 | tf_op jit(solution)/shard_map/ppermute | solution.py:17
  380.5 8.6 %collective-permute-start.3 = (f32[4,10,1,1024]{3,2,1,0:T(1,128)S(1)}, f32[4,10,1,1024]{3,2,1,0:T(1,128)S(1)}, u32[]{:S(2)}, u32[]{:S(2)}) collective-permute-start(f32[4,10,1,1024]{3,2,1,0:T(1,128)S(1)} %get-tuple-element.47), channel_id=1, source_target_pairs={{0,1},{1,2},{2,3},{3,4},{4,5},{5,6},{6,7},{8,9},{9,10},{10,11},{11... | collective-permute-start | bytes 491528 | tf_op jit(solution)/shard_map/ppermute | solution.py:16
  384.1 8.7 %collective-permute-start.2 = (f32[4,10,1,1024]{3,2,1,0:T(1,128)S(1)}, f32[4,10,1,1024]{3,2,1,0:T(1,128)S(1)}, u32[]{:S(2)}, u32[]{:S(2)}) collective-permute-start(f32[4,10,1,1024]{3,2,1,0:T(1,128)S(1)} %get-tuple-element.46), channel_id=1, source_target_pairs={{1,0},{2,1},{3,2},{4,3},{5,4},{6,5},{7,6},{9,8},{10,9},{11,10},{12... | collective-permute-start | bytes 491528 | tf_op jit(solution)/shard_map/ppermute | solution.py:17
  389.1 40.2 %collective-permute-start.30 = (bf16[4,10,1,1024]{3,2,1,0:T(2,128)(2,1)S(1)}, bf16[4,10,1,1024]{3,2,1,0:T(2,128)(2,1)S(1)}, u32[]{:S(2)}, u32[]{:S(2)}) collective-permute-start(bf16[4,10,1,1024]{3,2,1,0:T(2,128)(2,1)S(1)} %get-tuple-element.70), channel_id=1, source_target_pairs={{0,1},{1,2},{2,3},{3,4},{4,5},{5,6},{6,7},{8,9},{9,10},{10,11},{11... | collective-permute-start | bytes 245768 | tf_op jit(solution)/shard_map/ppermute | solution.py:16
  392.9 54.9 %collective-permute-start.43 = (bf16[4,10,1,1024]{3,2,1,0:T(2,128)(2,1)S(1)}, bf16[4,10,1,1024]{3,2,1,0:T(2,128)(2,1)S(1)}, u32[]{:S(2)}, u32[]{:S(2)}) collective-permute-start(bf16[4,10,1,1024]{3,2,1,0:T(2,128)(2,1)S(1)} %get-tuple-element.69), channel_id=1, source_target_pairs={{1,0},{2,1},{3,2},{4,3},{5,4},{6,5},{7,6},{9,8},{10,9},{11,10},{12... | collective-permute-start | bytes 245768 | tf_op jit(solution)/shard_map/ppermute | solution.py:17
  404.4 7.6 %collective-permute-start.11 = (f32[10,1,1024]{2,1,0:T(1,128)S(1)}, f32[10,1,1024]{2,1,0:T(1,128)S(1)}, u32[]{:S(2)}, u32[]{:S(2)}) collective-permute-start(f32[10,1,1024]{2,1,0:T(1,128)S(1)} %get-tuple-element.99), channel_id=1, source_target_pairs={{0,1},{1,2},{2,3},{3,4},{4,5},{5,6},{6,7},{8,9},{9,10},{10,11},{11... | collective-permute-start | bytes 122888 | tf_op jit(solution)/shard_map/ppermute | solution.py:16
  420.0 27.8 %collective-permute-start.42 = (bf16[4,10,1,1024]{3,2,1,0:T(2,128)(2,1)S(1)}, bf16[4,10,1,1024]{3,2,1,0:T(2,128)(2,1)S(1)}, u32[]{:S(2)}, u32[]{:S(2)}) collective-permute-start(bf16[4,10,1,1024]{3,2,1,0:T(2,128)(2,1)S(1)} %get-tuple-element.68), channel_id=1, source_target_pairs={{0,1},{1,2},{2,3},{3,4},{4,5},{5,6},{6,7},{8,9},{9,10},{10,11},{11... | collective-permute-start | bytes 245768 | tf_op jit(solution)/shard_map/ppermute | solution.py:16
  460.3 6.7 %collective-permute-start.27 = (f32[4,10,1,1024]{3,2,1,0:T(1,128)S(1)}, f32[4,10,1,1024]{3,2,1,0:T(1,128)S(1)}, u32[]{:S(2)}, u32[]{:S(2)}) collective-permute-start(f32[4,10,1,1024]{3,2,1,0:T(1,128)S(1)} %get-tuple-element.39), channel_id=1, source_target_pairs={{0,1},{1,2},{2,3},{3,4},{4,5},{5,6},{6,7},{8,9},{9,10},{10,11},{11... | collective-permute-start | bytes 491528 | tf_op jit(solution)/shard_map/ppermute | solution.py:16
  463.7 6.6 %collective-permute-start.26 = (f32[4,10,1,1024]{3,2,1,0:T(1,128)S(1)}, f32[4,10,1,1024]{3,2,1,0:T(1,128)S(1)}, u32[]{:S(2)}, u32[]{:S(2)}) collective-permute-start(f32[4,10,1,1024]{3,2,1,0:T(1,128)S(1)} %get-tuple-element.38), channel_id=1, source_target_pairs={{1,0},{2,1},{3,2},{4,3},{5,4},{6,5},{7,6},{9,8},{10,9},{11,10},{12... | collective-permute-start | bytes 491528 | tf_op jit(solution)/shard_map/ppermute | solution.py:17
  (33 other events, 222.1 us)
Sparse Core Ops, SparseCore 0:
  527.4 21.7 reduce-scatter.1
where the time goes:
time: 559 us; the launch traced here: 556 us
  blocking collectives  279 us (50%)
  starting transfers between devices  124 us (22%)
  waiting for transfers between devices  64.3 us (12%)
  other arithmetic  39.6 us (7%)
  local copies, waits for them, and re-layouts  33.9 us (6%)
  between operations  15.8 us (3%)
    psum x1, blocking collectives, shards(): samples = lax.psum(local_samples, ('gx', 'gy'))  279 us
    ppermute x24, starting transfers between devices, extended(): before = lax.ppermute(last, axis, up)  76.4 us
    ppermute x24, starting transfers between devices, extended(): after = lax.ppermute(initial, axis, down)  47.4 us
    ppermute x24, waiting for transfers between devices, extended(): after = lax.ppermute(initial, axis, down)  42.7 us
    reduce_scatter x1, waiting for transfers between devices, shards(): lax.psum_scatter(kernel_local, 'pair', scatter_dimension=3, tiled=True)  20.9 us
    slice x2, local copies, waits for them, and re-layouts, shards(): pressure_snaps = forward_field[:, 0].reshape(steps_total, -1)  14.9 us
  transfers between devices with their start and end apart: 49, of which 18 were waited for; matrix products, arithmetic and copies ran while one was open for 11% of the time, Pallas kernels for 0%

commit v1 on v0

--- a/solution.py
+++ b/solution.py
@@ -2,6 +2,7 @@
 import jax.numpy as jnp
 from jax import lax
 from jax.sharding import PartitionSpec as P
+from jax.lax import psum
 
 step_length = 0.25
 
@@ -62,7 +63,7 @@
     local_samples = (
         jnp.take(pressure_snaps, src_flat, axis=1).astype(jnp.float32) * src_inside[None, :]
     )
-    samples = lax.psum(local_samples, ("gx", "gy"))
+    samples = psum(psum(local_samples, "gx"), "gy")
     state = adjoint_state[0]
     kernel_local = jnp.zeros((4, width_x, width_y, depth), jnp.float32)
     for step in range(steps_total):

time: 559 us -> 347 us (0.62)
  blocking collectives: 279 us -> 64.4 us
    psum x1 -> x2, blocking collectives: 279 us -> 64.4 us  [shards(): samples = psum(psum(local_samples, 'gx'), 'gy')]
    ppermute x24, starting transfers between devices: 76.4 us -> 82.8 us  [extended(): before = lax.ppermute(last, axis, up)]
  transfers between devices with their start and end apart: 49 -> 49, of which waited for: 18 -> 18; matrix products, arithmetic and copies ran while one was open for 11% -> 19% of each run, Pallas kernels for 0% -> 0%
where the time goes in v1:
time: 347 us; the launch traced here: 344 us
  starting transfers between devices  127 us (37%)
  blocking collectives  64.4 us (19%)
  waiting for transfers between devices  63 us (18%)
  other arithmetic  39.7 us (11%)
  local copies, waits for them, and re-layouts  34 us (10%)
  between operations  15.8 us (5%)
    ppermute x24, starting transfers between devices, extended(): before = lax.ppermute(last, axis, up)  82.8 us
    psum x2, blocking collectives, shards(): samples = psum(psum(local_samples, 'gx'), 'gy')  64.4 us
    ppermute x24, starting transfers between devices, extended(): after = lax.ppermute(initial, axis, down)  44 us
    ppermute x24, waiting for transfers between devices, extended(): after = lax.ppermute(initial, axis, down)  43.3 us
    reduce_scatter x1, waiting for transfers between devices, shards(): lax.psum_scatter(kernel_local, 'pair', scatter_dimension=3, tiled=True)  19 us
    slice x2, local copies, waits for them, and re-layouts, shards(): pressure_snaps = forward_field[:, 0].reshape(steps_total, -1)  15 us
    scatter-add x4, other arithmetic, shards(): injected = jnp.zeros((width_x * width_y * depth,), jnp.float32).at[rcv_fl...  9.35 us
    gather x1, local copies, waits for them, and re-layouts, shards(): jnp.take(pressure_snaps, src_flat, axis=1).astype(jnp.float32)  8.65 us
  transfers between devices with their start and end apart: 49, of which 18 were waited for; matrix products, arithmetic and copies ran while one was open for 19% of the time, Pallas kernels for 0%

profile of v1, /device:TPU:1, one launch (start us, length us, event | category | flops | bytes accessed | tf_op | source)
XLA Modules:
  0.0 343.7 jit_solution(17728707361067257529)
XLA Ops:
  11.0 5.2 %collective-permute-start.4 = (bf16[4,1,8,1024]{3,2,1,0:T(8,128)(2,1)}, bf16[4,1,8,1024]{3,2,1,0:T(8,128)(2,1)}, u32[]{:S(2)}, u32[]{:S(2)}) collective-permute-start(bf16[4,1,8,1024]{3,2,1,0:T(8,128)(2,1)} %get-tuple-element.82), channel_id=1, source_target_pairs={{0,8},{8,16},{16,24},{24,32},{32,40},{40,48},{48,56},{1,9},{9,17},... | collective-permute-start | bytes 196616 | tf_op jit(solution)/shard_map/ppermute | solution.py:17
  17.0 3.6 %collective-permute-start.1 = (f32[4,1,8,1024]{3,2,1,0:T(8,128)}, f32[4,1,8,1024]{3,2,1,0:T(8,128)S(1)}, u32[]{:S(2)}, u32[]{:S(2)}) collective-permute-start(f32[4,1,8,1024]{3,2,1,0:T(8,128)} %get-tuple-element.66), channel_id=1, source_target_pairs={{0,8},{8,16},{16,24},{24,32},{32,40},{40,48},{48,56},{1,9},{9,17},... | collective-permute-start | bytes 393224 | tf_op jit(solution)/shard_map/ppermute | solution.py:17
  26.9 13.2 %copy.11 = bf16[4,1,8,8,1024]{0,4,3,2,1:T(8,128)(2,1)} copy(bf16[4,1,8,8,1024]{4,3,2,1,0:T(8,128)(2,1)} %slice.831) | data formatting | bytes 1048576 | tf_op jit(solution)/shard_map/slice | solution.py:62
  40.1 8.7 %gather_fusion = bf16[256,4]{1,0:T(8,128)(2,1)S(1)} fusion(bf16[4,65536]{0,1:T(8,128)(2,1)} %bitcast.532, s32[1024]{0:T(1024)S(1)} %pad_clamp_fusion), kind=kCustom, calls=%fused_computation | custom fusion | bytes 5120 | tf_op jit(solution)/shard_map/jit(_take)/gather | solution.py:64
  48.9 32.7 %psum.14 = f32[4,256]{0,1:T(8,128)S(1)} all-reduce(f32[4,256]{0,1:T(8,128)S(1)} %multiply_bitcast_fusion), channel_id=1, replica_groups=mesh['pair'=2,'gx'=8,'gy'=8] {'gx'}, use_global_device_ids=true, to_apply=%region_0.1 | all-reduce | flops 1024 | bytes 8192 | tf_op jit(solution)/shard_map/psum | solution.py:66
  81.6 31.7 %psum.15 = f32[4,256]{0,1:T(8,128)S(1)} all-reduce(f32[4,256]{0,1:T(8,128)S(1)} %psum.14), channel_id=1, replica_groups=mesh['pair'=2,'gx'=8,'gy'=8] {'gy'}, use_global_device_ids=true, to_apply=%region_1.2 | all-reduce | flops 1024 | bytes 8192 | tf_op jit(solution)/shard_map/psum | solution.py:66
  134.9 4.0 %collective-permute-start.28 = (bf16[4,1,8,1024]{3,2,1,0:T(8,128)(2,1)}, bf16[4,1,8,1024]{3,2,1,0:T(8,128)(2,1)S(1)}, u32[]{:S(2)}, u32[]{:S(2)}) collective-permute-start(bf16[4,1,8,1024]{3,2,1,0:T(8,128)(2,1)} %get-tuple-element.78), channel_id=1, source_target_pairs={{0,8},{8,16},{16,24},{24,32},{32,40},{40,48},{48,56},{1,9},{9,17},... | collective-permute-start | bytes 196616 | tf_op jit(solution)/shard_map/ppermute | solution.py:17
  141.3 4.0 %collective-permute-start.40 = (bf16[4,1,8,1024]{3,2,1,0:T(8,128)(2,1)}, bf16[4,1,8,1024]{3,2,1,0:T(8,128)(2,1)S(1)}, u32[]{:S(2)}, u32[]{:S(2)}) collective-permute-start(bf16[4,1,8,1024]{3,2,1,0:T(8,128)(2,1)} %get-tuple-element.76), channel_id=1, source_target_pairs={{0,8},{8,16},{16,24},{24,32},{32,40},{40,48},{48,56},{1,9},{9,17},... | collective-permute-start | bytes 196616 | tf_op jit(solution)/shard_map/ppermute | solution.py:17
  145.3 6.5 %collective-permute-start.7 = (bf16[4,10,1,1024]{3,2,1,0:T(2,128)(2,1)S(1)}, bf16[4,10,1,1024]{3,2,1,0:T(2,128)(2,1)S(1)}, u32[]{:S(2)}, u32[]{:S(2)}) collective-permute-start(bf16[4,10,1,1024]{3,2,1,0:T(2,128)(2,1)S(1)} %get-tuple-element.75), channel_id=1, source_target_pairs={{1,0},{2,1},{3,2},{4,3},{5,4},{6,5},{7,6},{9,8},{10,9},{11,10},{12... | collective-permute-start | bytes 245768 | tf_op jit(solution)/shard_map/ppermute | solution.py:18
  163.0 3.6 %collective-permute-start.3 = (f32[4,10,1,1024]{3,2,1,0:T(1,128)S(1)}, f32[4,10,1,1024]{3,2,1,0:T(1,128)S(1)}, u32[]{:S(2)}, u32[]{:S(2)}) collective-permute-start(f32[4,10,1,1024]{3,2,1,0:T(1,128)S(1)} %get-tuple-element.47), channel_id=1, source_target_pairs={{0,1},{1,2},{2,3},{3,4},{4,5},{5,6},{6,7},{8,9},{9,10},{10,11},{11... | collective-permute-start | bytes 491528 | tf_op jit(solution)/shard_map/ppermute | solution.py:17
  171.6 3.8 %collective-permute-start.30 = (bf16[4,10,1,1024]{3,2,1,0:T(2,128)(2,1)S(1)}, bf16[4,10,1,1024]{3,2,1,0:T(2,128)(2,1)S(1)}, u32[]{:S(2)}, u32[]{:S(2)}) collective-permute-start(bf16[4,10,1,1024]{3,2,1,0:T(2,128)(2,1)S(1)} %get-tuple-element.70), channel_id=1, source_target_pairs={{0,1},{1,2},{2,3},{3,4},{4,5},{5,6},{6,7},{8,9},{9,10},{10,11},{11... | collective-permute-start | bytes 245768 | tf_op jit(solution)/shard_map/ppermute | solution.py:17
  179.6 4.3 %collective-permute-start.9 = (f32[1,8,1024]{2,1,0:T(8,128)S(1)}, f32[1,8,1024]{2,1,0:T(8,128)S(1)}, u32[]{:S(2)}, u32[]{:S(2)}) collective-permute-start(f32[1,8,1024]{2,1,0:T(8,128)S(1)} %get-tuple-element.110), channel_id=1, source_target_pairs={{0,8},{8,16},{16,24},{24,32},{32,40},{40,48},{48,56},{1,9},{9,17},... | collective-permute-start | bytes 98312 | tf_op jit(solution)/shard_map/ppermute | solution.py:17
  188.6 5.1 %collective-permute-start.11 = (f32[10,1,1024]{2,1,0:T(1,128)S(1)}, f32[10,1,1024]{2,1,0:T(1,128)S(1)}, u32[]{:S(2)}, u32[]{:S(2)}) collective-permute-start(f32[10,1,1024]{2,1,0:T(1,128)S(1)} %get-tuple-element.99), channel_id=1, source_target_pairs={{0,1},{1,2},{2,3},{3,4},{4,5},{5,6},{6,7},{8,9},{9,10},{10,11},{11... | collective-permute-start | bytes 122888 | tf_op jit(solution)/shard_map/ppermute | solution.py:17
  208.3 3.3 collective-permute-start.15
  214.2 4.0 %collective-permute-done.14 = f32[4,10,1,1024]{3,2,1,0:T(1,128)S(1)} collective-permute-done((f32[4,10,1,1024]{3,2,1,0:T(1,128)S(1)}, f32[4,10,1,1024]{3,2,1,0:T(1,128)S(1)}, u32[]{:S(2)}, u32[]{:S(2)}) %collective-permute-start.14) | collective-permute-done | bytes 163872 | tf_op jit(solution)/shard_map/ppermute | solution.py:18
  219.6 3.6 %collective-permute-start.21 = (f32[1,8,1024]{2,1,0:T(8,128)S(1)}, f32[1,8,1024]{2,1,0:T(8,128)S(1)}, u32[]{:S(2)}, u32[]{:S(2)}) collective-permute-start(f32[1,8,1024]{2,1,0:T(8,128)S(1)} %get-tuple-element.107), channel_id=1, source_target_pairs={{0,8},{8,16},{16,24},{24,32},{32,40},{40,48},{48,56},{1,9},{9,17},... | collective-permute-start | bytes 98312 | tf_op jit(solution)/shard_map/ppermute | solution.py:17
  237.2 4.3 %collective-permute-start.25 = (f32[4,1,8,1024]{3,2,1,0:T(8,128)S(1)}, f32[4,1,8,1024]{3,2,1,0:T(8,128)S(1)}, u32[]{:S(2)}, u32[]{:S(2)}) collective-permute-start(f32[4,1,8,1024]{3,2,1,0:T(8,128)S(1)} %get-tuple-element.56), channel_id=1, source_target_pairs={{0,8},{8,16},{16,24},{24,32},{32,40},{40,48},{48,56},{1,9},{9,17},... | collective-permute-start | bytes 393224 | tf_op jit(solution)/shard_map/ppermute | solution.py:17
  243.4 4.3 %collective-permute-done.24 = f32[4,1,8,1024]{3,2,1,0:T(8,128)S(1)} collective-permute-done((f32[4,1,8,1024]{3,2,1,0:T(8,128)S(1)}, f32[4,1,8,1024]{3,2,1,0:T(8,128)S(1)}, u32[]{:S(2)}, u32[]{:S(2)}) %collective-permute-start.24) | collective-permute-done | bytes 131104 | tf_op jit(solution)/shard_map/ppermute | solution.py:18
  259.1 3.9 %collective-permute-start.33 = (f32[1,8,1024]{2,1,0:T(8,128)S(1)}, f32[1,8,1024]{2,1,0:T(8,128)S(1)}, u32[]{:S(2)}, u32[]{:S(2)}) collective-permute-start(f32[1,8,1024]{2,1,0:T(8,128)S(1)} %get-tuple-element.104), channel_id=1, source_target_pairs={{0,8},{8,16},{16,24},{24,32},{32,40},{40,48},{48,56},{1,9},{9,17},... | collective-permute-start | bytes 98312 | tf_op jit(solution)/shard_map/ppermute | solution.py:17
  276.9 3.5 %collective-permute-start.37 = (f32[4,1,8,1024]{3,2,1,0:T(8,128)S(1)}, f32[4,1,8,1024]{3,2,1,0:T(8,128)S(1)}, u32[]{:S(2)}, u32[]{:S(2)}) collective-permute-start(f32[4,1,8,1024]{3,2,1,0:T(8,128)S(1)} %get-tuple-element.51), channel_id=1, source_target_pairs={{0,8},{8,16},{16,24},{24,32},{32,40},{40,48},{48,56},{1,9},{9,17},... | collective-permute-start | bytes 393224 | tf_op jit(solution)/shard_map/ppermute | solution.py:17
  282.4 3.8 %collective-permute-done.36 = f32[4,1,8,1024]{3,2,1,0:T(8,128)S(1)} collective-permute-done((f32[4,1,8,1024]{3,2,1,0:T(8,128)S(1)}, f32[4,1,8,1024]{3,2,1,0:T(8,128)S(1)}, u32[]{:S(2)}, u32[]{:S(2)}) %collective-permute-start.36) | collective-permute-done | bytes 131104 | tf_op jit(solution)/shard_map/ppermute | solution.py:18
  286.3 3.7 %collective-permute-start.39 = (f32[4,10,1,1024]{3,2,1,0:T(1,128)S(1)}, f32[4,10,1,1024]{3,2,1,0:T(1,128)S(1)}, u32[]{:S(2)}, u32[]{:S(2)}) collective-permute-start(f32[4,10,1,1024]{3,2,1,0:T(1,128)S(1)} %get-tuple-element.35), channel_id=1, source_target_pairs={{0,1},{1,2},{2,3},{3,4},{4,5},{5,6},{6,7},{8,9},{9,10},{10,11},{11... | collective-permute-start | bytes 491528 | tf_op jit(solution)/shard_map/ppermute | solution.py:17
  292.3 4.4 %collective-permute-done.38 = f32[4,10,1,1024]{3,2,1,0:T(1,128)S(1)} collective-permute-done((f32[4,10,1,1024]{3,2,1,0:T(1,128)S(1)}, f32[4,10,1,1024]{3,2,1,0:T(1,128)S(1)}, u32[]{:S(2)}, u32[]{:S(2)}) %collective-permute-start.38) | collective-permute-done | bytes 163872 | tf_op jit(solution)/shard_map/ppermute | solution.py:18
  317.9 19.0 %reduce-scatter.2.cloned.1.call-done = f32[4,8,8,512]{3,2,1,0:T(8,128)} async-done(((f32[4,8,8,1024]{3,2,1,0:T(8,128)}), f32[4,8,8,512]{3,2,1,0:T(8,128)}) %reduce-scatter.2.cloned.1.call-update) | async-done | bytes 524304 | tf_op jit(solution)/shard_map/reduce_scatter | solution.py:113
  (179 shorter events, 143.9 us)
Async XLA Ops:
  7.2 329.7 %reduce-scatter.2.cloned.1.call-start = ((), (), s32[]{:S(2)}) async-start(), calls=%async_computation.1 | async-start | bytes 1572864 | tf_op jit(solution)/shard_map/reduce_scatter | solution.py:113
  9.8 121.3 %collective-permute-start.5 = (bf16[4,1,8,1024]{3,2,1,0:T(8,128)(2,1)}, bf16[4,1,8,1024]{3,2,1,0:T(8,128)(2,1)}, u32[]{:S(2)}, u32[]{:S(2)}) collective-permute-start(bf16[4,1,8,1024]{3,2,1,0:T(8,128)(2,1)} %get-tuple-element.83), channel_id=1, source_target_pairs={{8,0},{16,8},{24,16},{32,24},{40,32},{48,40},{56,48},{9,1},{17,9},... | collective-permute-start | bytes 196616 | tf_op jit(solution)/shard_map/ppermute | solution.py:18
  11.0 121.3 %collective-permute-start.4 = (bf16[4,1,8,1024]{3,2,1,0:T(8,128)(2,1)}, bf16[4,1,8,1024]{3,2,1,0:T(8,128)(2,1)}, u32[]{:S(2)}, u32[]{:S(2)}) collective-permute-start(bf16[4,1,8,1024]{3,2,1,0:T(8,128)(2,1)} %get-tuple-element.82), channel_id=1, source_target_pairs={{0,8},{8,16},{16,24},{24,32},{32,40},{40,48},{48,56},{1,9},{9,17},... | collective-permute-start | bytes 196616 | tf_op jit(solution)/shard_map/ppermute | solution.py:17
  17.0 139.7 %collective-permute-start.1 = (f32[4,1,8,1024]{3,2,1,0:T(8,128)}, f32[4,1,8,1024]{3,2,1,0:T(8,128)S(1)}, u32[]{:S(2)}, u32[]{:S(2)}) collective-permute-start(f32[4,1,8,1024]{3,2,1,0:T(8,128)} %get-tuple-element.66), channel_id=1, source_target_pairs={{0,8},{8,16},{16,24},{24,32},{32,40},{40,48},{48,56},{1,9},{9,17},... | collective-permute-start | bytes 393224 | tf_op jit(solution)/shard_map/ppermute | solution.py:17
  20.6 139.2 %collective-permute-start = (f32[4,1,8,1024]{3,2,1,0:T(8,128)}, f32[4,1,8,1024]{3,2,1,0:T(8,128)}, u32[]{:S(2)}, u32[]{:S(2)}) collective-permute-start(f32[4,1,8,1024]{3,2,1,0:T(8,128)} %get-tuple-element.67), channel_id=1, source_target_pairs={{8,0},{16,8},{24,16},{32,24},{40,32},{48,40},{56,48},{9,1},{17,9},... | collective-permute-start | bytes 393224 | tf_op jit(solution)/shard_map/ppermute | solution.py:18
  22.6 112.2 %collective-permute-start.17 = (bf16[4,1,8,1024]{3,2,1,0:T(8,128)(2,1)}, bf16[4,1,8,1024]{3,2,1,0:T(8,128)(2,1)}, u32[]{:S(2)}, u32[]{:S(2)}) collective-permute-start(bf16[4,1,8,1024]{3,2,1,0:T(8,128)(2,1)} %get-tuple-element.81), channel_id=1, source_target_pairs={{8,0},{16,8},{24,16},{32,24},{40,32},{48,40},{56,48},{9,1},{17,9},... | collective-permute-start | bytes 196616 | tf_op jit(solution)/shard_map/ppermute | solution.py:18
  131.1 7.8 %collective-permute-start.16 = (bf16[4,1,8,1024]{3,2,1,0:T(8,128)(2,1)}, bf16[4,1,8,1024]{3,2,1,0:T(8,128)(2,1)S(1)}, u32[]{:S(2)}, u32[]{:S(2)}) collective-permute-start(bf16[4,1,8,1024]{3,2,1,0:T(8,128)(2,1)} %get-tuple-element.80), channel_id=1, source_target_pairs={{0,8},{8,16},{16,24},{24,32},{32,40},{40,48},{48,56},{1,9},{9,17},... | collective-permute-start | bytes 196616 | tf_op jit(solution)/shard_map/ppermute | solution.py:17
  132.4 8.9 %collective-permute-start.29 = (bf16[4,1,8,1024]{3,2,1,0:T(8,128)(2,1)}, bf16[4,1,8,1024]{3,2,1,0:T(8,128)(2,1)S(1)}, u32[]{:S(2)}, u32[]{:S(2)}) collective-permute-start(bf16[4,1,8,1024]{3,2,1,0:T(8,128)(2,1)} %get-tuple-element.79), channel_id=1, source_target_pairs={{8,0},{16,8},{24,16},{32,24},{40,32},{48,40},{56,48},{9,1},{17,9},... | collective-permute-start | bytes 196616 | tf_op jit(solution)/shard_map/ppermute | solution.py:18
  134.9 10.5 %collective-permute-start.28 = (bf16[4,1,8,1024]{3,2,1,0:T(8,128)(2,1)}, bf16[4,1,8,1024]{3,2,1,0:T(8,128)(2,1)S(1)}, u32[]{:S(2)}, u32[]{:S(2)}) collective-permute-start(bf16[4,1,8,1024]{3,2,1,0:T(8,128)(2,1)} %get-tuple-element.78), channel_id=1, source_target_pairs={{0,8},{8,16},{16,24},{24,32},{32,40},{40,48},{48,56},{1,9},{9,17},... | collective-permute-start | bytes 196616 | tf_op jit(solution)/shard_map/ppermute | solution.py:17
  138.9 13.2 %collective-permute-start.41 = (bf16[4,1,8,1024]{3,2,1,0:T(8,128)(2,1)}, bf16[4,1,8,1024]{3,2,1,0:T(8,128)(2,1)S(1)}, u32[]{:S(2)}, u32[]{:S(2)}) collective-permute-start(bf16[4,1,8,1024]{3,2,1,0:T(8,128)(2,1)} %get-tuple-element.77), channel_id=1, source_target_pairs={{8,0},{16,8},{24,16},{32,24},{40,32},{48,40},{56,48},{9,1},{17,9},... | collective-permute-start | bytes 196616 | tf_op jit(solution)/shard_map/ppermute | solution.py:18
  141.3 12.7 %collective-permute-start.40 = (bf16[4,1,8,1024]{3,2,1,0:T(8,128)(2,1)}, bf16[4,1,8,1024]{3,2,1,0:T(8,128)(2,1)S(1)}, u32[]{:S(2)}, u32[]{:S(2)}) collective-permute-start(bf16[4,1,8,1024]{3,2,1,0:T(8,128)(2,1)} %get-tuple-element.76), channel_id=1, source_target_pairs={{0,8},{8,16},{16,24},{24,32},{32,40},{40,48},{48,56},{1,9},{9,17},... | collective-permute-start | bytes 196616 | tf_op jit(solution)/shard_map/ppermute | solution.py:17
  145.3 17.6 %collective-permute-start.7 = (bf16[4,10,1,1024]{3,2,1,0:T(2,128)(2,1)S(1)}, bf16[4,10,1,1024]{3,2,1,0:T(2,128)(2,1)S(1)}, u32[]{:S(2)}, u32[]{:S(2)}) collective-permute-start(bf16[4,10,1,1024]{3,2,1,0:T(2,128)(2,1)S(1)} %get-tuple-element.75), channel_id=1, source_target_pairs={{1,0},{2,1},{3,2},{4,3},{5,4},{6,5},{7,6},{9,8},{10,9},{11,10},{12... | collective-permute-start | bytes 245768 | tf_op jit(solution)/shard_map/ppermute | solution.py:18
  152.1 14.5 %collective-permute-start.6 = (bf16[4,10,1,1024]{3,2,1,0:T(2,128)(2,1)S(1)}, bf16[4,10,1,1024]{3,2,1,0:T(2,128)(2,1)S(1)}, u32[]{:S(2)}, u32[]{:S(2)}) collective-permute-start(bf16[4,10,1,1024]{3,2,1,0:T(2,128)(2,1)S(1)} %get-tuple-element.74), channel_id=1, source_target_pairs={{0,1},{1,2},{2,3},{3,4},{4,5},{5,6},{6,7},{8,9},{9,10},{10,11},{11... | collective-permute-start | bytes 245768 | tf_op jit(solution)/shard_map/ppermute | solution.py:17
  154.0 25.6 %collective-permute-start.19 = (bf16[4,10,1,1024]{3,2,1,0:T(2,128)(2,1)S(1)}, bf16[4,10,1,1024]{3,2,1,0:T(2,128)(2,1)S(1)}, u32[]{:S(2)}, u32[]{:S(2)}) collective-permute-start(bf16[4,10,1,1024]{3,2,1,0:T(2,128)(2,1)S(1)} %get-tuple-element.73), channel_id=1, source_target_pairs={{1,0},{2,1},{3,2},{4,3},{5,4},{6,5},{7,6},{9,8},{10,9},{11,10},{12... | collective-permute-start | bytes 245768 | tf_op jit(solution)/shard_map/ppermute | solution.py:18
  156.7 27.2 %collective-permute-start.18 = (bf16[4,10,1,1024]{3,2,1,0:T(2,128)(2,1)S(1)}, bf16[4,10,1,1024]{3,2,1,0:T(2,128)(2,1)S(1)}, u32[]{:S(2)}, u32[]{:S(2)}) collective-permute-start(bf16[4,10,1,1024]{3,2,1,0:T(2,128)(2,1)S(1)} %get-tuple-element.72), channel_id=1, source_target_pairs={{0,1},{1,2},{2,3},{3,4},{4,5},{5,6},{6,7},{8,9},{9,10},{10,11},{11... | collective-permute-start | bytes 245768 | tf_op jit(solution)/shard_map/ppermute | solution.py:17
  159.8 51.7 %collective-permute-start.31 = (bf16[4,10,1,1024]{3,2,1,0:T(2,128)(2,1)S(1)}, bf16[4,10,1,1024]{3,2,1,0:T(2,128)(2,1)S(1)}, u32[]{:S(2)}, u32[]{:S(2)}) collective-permute-start(bf16[4,10,1,1024]{3,2,1,0:T(2,128)(2,1)S(1)} %get-tuple-element.71), channel_id=1, source_target_pairs={{1,0},{2,1},{3,2},{4,3},{5,4},{6,5},{7,6},{9,8},{10,9},{11,10},{12... | collective-permute-start | bytes 245768 | tf_op jit(solution)/shard_map/ppermute | solution.py:18
  163.0 8.6 %collective-permute-start.3 = (f32[4,10,1,1024]{3,2,1,0:T(1,128)S(1)}, f32[4,10,1,1024]{3,2,1,0:T(1,128)S(1)}, u32[]{:S(2)}, u32[]{:S(2)}) collective-permute-start(f32[4,10,1,1024]{3,2,1,0:T(1,128)S(1)} %get-tuple-element.47), channel_id=1, source_target_pairs={{0,1},{1,2},{2,3},{3,4},{4,5},{5,6},{6,7},{8,9},{9,10},{10,11},{11... | collective-permute-start | bytes 491528 | tf_op jit(solution)/shard_map/ppermute | solution.py:17
  166.6 8.7 %collective-permute-start.2 = (f32[4,10,1,1024]{3,2,1,0:T(1,128)S(1)}, f32[4,10,1,1024]{3,2,1,0:T(1,128)S(1)}, u32[]{:S(2)}, u32[]{:S(2)}) collective-permute-start(f32[4,10,1,1024]{3,2,1,0:T(1,128)S(1)} %get-tuple-element.46), channel_id=1, source_target_pairs={{1,0},{2,1},{3,2},{4,3},{5,4},{6,5},{7,6},{9,8},{10,9},{11,10},{12... | collective-permute-start | bytes 491528 | tf_op jit(solution)/shard_map/ppermute | solution.py:18
  171.6 41.9 %collective-permute-start.30 = (bf16[4,10,1,1024]{3,2,1,0:T(2,128)(2,1)S(1)}, bf16[4,10,1,1024]{3,2,1,0:T(2,128)(2,1)S(1)}, u32[]{:S(2)}, u32[]{:S(2)}) collective-permute-start(bf16[4,10,1,1024]{3,2,1,0:T(2,128)(2,1)S(1)} %get-tuple-element.70), channel_id=1, source_target_pairs={{0,1},{1,2},{2,3},{3,4},{4,5},{5,6},{6,7},{8,9},{9,10},{10,11},{11... | collective-permute-start | bytes 245768 | tf_op jit(solution)/shard_map/ppermute | solution.py:17
  175.4 57.7 %collective-permute-start.43 = (bf16[4,10,1,1024]{3,2,1,0:T(2,128)(2,1)S(1)}, bf16[4,10,1,1024]{3,2,1,0:T(2,128)(2,1)S(1)}, u32[]{:S(2)}, u32[]{:S(2)}) collective-permute-start(bf16[4,10,1,1024]{3,2,1,0:T(2,128)(2,1)S(1)} %get-tuple-element.69), channel_id=1, source_target_pairs={{1,0},{2,1},{3,2},{4,3},{5,4},{6,5},{7,6},{9,8},{10,9},{11,10},{12... | collective-permute-start | bytes 245768 | tf_op jit(solution)/shard_map/ppermute | solution.py:18
  179.6 7.1 %collective-permute-start.9 = (f32[1,8,1024]{2,1,0:T(8,128)S(1)}, f32[1,8,1024]{2,1,0:T(8,128)S(1)}, u32[]{:S(2)}, u32[]{:S(2)}) collective-permute-start(f32[1,8,1024]{2,1,0:T(8,128)S(1)} %get-tuple-element.110), channel_id=1, source_target_pairs={{0,8},{8,16},{16,24},{24,32},{32,40},{40,48},{48,56},{1,9},{9,17},... | collective-permute-start | bytes 98312 | tf_op jit(solution)/shard_map/ppermute | solution.py:17
  188.6 7.6 %collective-permute-start.11 = (f32[10,1,1024]{2,1,0:T(1,128)S(1)}, f32[10,1,1024]{2,1,0:T(1,128)S(1)}, u32[]{:S(2)}, u32[]{:S(2)}) collective-permute-start(f32[10,1,1024]{2,1,0:T(1,128)S(1)} %get-tuple-element.99), channel_id=1, source_target_pairs={{0,1},{1,2},{2,3},{3,4},{4,5},{5,6},{6,7},{8,9},{9,10},{10,11},{11... | collective-permute-start | bytes 122888 | tf_op jit(solution)/shard_map/ppermute | solution.py:17
  204.2 28.8 %collective-permute-start.42 = (bf16[4,10,1,1024]{3,2,1,0:T(2,128)(2,1)S(1)}, bf16[4,10,1,1024]{3,2,1,0:T(2,128)(2,1)S(1)}, u32[]{:S(2)}, u32[]{:S(2)}) collective-permute-start(bf16[4,10,1,1024]{3,2,1,0:T(2,128)(2,1)S(1)} %get-tuple-element.68), channel_id=1, source_target_pairs={{0,1},{1,2},{2,3},{3,4},{4,5},{5,6},{6,7},{8,9},{9,10},{10,11},{11... | collective-permute-start | bytes 245768 | tf_op jit(solution)/shard_map/ppermute | solution.py:17
  211.6 6.6 %collective-permute-start.14 = (f32[4,10,1,1024]{3,2,1,0:T(1,128)S(1)}, f32[4,10,1,1024]{3,2,1,0:T(1,128)S(1)}, u32[]{:S(2)}, u32[]{:S(2)}) collective-permute-start(f32[4,10,1,1024]{3,2,1,0:T(1,128)S(1)} %get-tuple-element.42), channel_id=1, source_target_pairs={{1,0},{2,1},{3,2},{4,3},{5,4},{6,5},{7,6},{9,8},{10,9},{11,10},{12... | collective-permute-start | bytes 491528 | tf_op jit(solution)/shard_map/ppermute | solution.py:18
  (33 other events, 228.8 us)
Sparse Core Ops, SparseCore 0:
  317.0 19.8 reduce-scatter.1
